TPU v7x, 32 devices: a whole 2x2x4 slice. The times are simulated.
32 devices in a mesh: client: 4 (over z), expert: 4 (over y, x), shard: 2 (over core).
Axes of the slice: x: 2, y: 2, z: 4, core: 2. Of those that a mesh axis runs over, the one named last changes fastest.
Arguments:
- tokens: bfloat16 [4, 512, 2048], P('client', 'expert'), may hold values from -6 to 6
- target: bfloat16 [4, 512, 2048], P('client', 'expert'), may hold values from -6 to 6
- routes: int32 [4, 512, 2], P('client', 'expert'), may hold values from 0 to 7, all different within a row; in each aligned block of 128 rows (0 to 127, 128 to 255, ..., all dimensions but the last counted through in order) at most 32 rows name the same one
- gate_weights: float32 [4, 512, 2], P('client', 'expert'), may hold values from 0.1 to 1
- counts: int32 [4], replicated, may hold values from 128 to 512
- gate_proj: bfloat16 [57344, 2048], P(('expert', 'shard'), 'client'), may hold values from -0.125 to 0.125
- up_proj: bfloat16 [57344, 2048], P(('expert', 'shard'), 'client'), may hold values from -0.125 to 0.125
- down_proj: bfloat16 [57344, 2048], P(('expert', 'shard'), 'client'), may hold values from -0.0625 to 0.0625
- correction: bfloat16 [4, 57344, 2048], P('client', ('expert', 'shard')), may hold values from -6 to 6
Outputs:
- pseudo_gradient: float32 [57344, 2048], P(('expert', 'shard'), 'client')
Inputs may be any that keep to these rules, and one draw needn't show every extreme that they name: `routes`: in each aligned block of 128 rows of a client, every expert is named by exactly 32 rows; the 2 ids of a row differ.
All inputs are finite; a program needn't handle non-finite values.
Results may differ from a plain program's by a relative error of at most 0.015.
Values may be sent and summed in bfloat16 or wider, within the bound.
A program may use at most 256 MiB of HBM per device.

v0:
```python
import jax
import jax.numpy as jnp
from jax import lax
from jax.sharding import PartitionSpec as P

FF = 7168
EXPERTS = 8
LOCAL_STEPS = 2


def local(tokens, target, routes, gate_weights, counts, gate_proj, up_proj, down_proj, correction):
    expert_count = lax.axis_size("expert")
    shard_count = lax.axis_size("shard")
    client_count = lax.axis_size("client")
    expert_index = lax.axis_index("expert")
    shard_index = lax.axis_index("shard")
    client_index = lax.axis_index("client")
    unit_count = down_proj.shape[0]
    token_count = tokens.shape[1]
    top_count = routes.shape[2]
    feature_width = tokens.shape[2]
    capacity = token_count * top_count // EXPERTS
    per_index = shard_count * unit_count
    hosted = max(1, per_index // FF)
    copies = max(1, FF // per_index)
    own_expert = (expert_index * shard_count + shard_index) * unit_count // FF
    first_expert = expert_index * per_index // FF
    offset = (own_expert - first_expert) * capacity
    flat_routes = routes[0].reshape(-1)
    onehot = (flat_routes[:, None] == jnp.arange(EXPERTS, dtype=jnp.int32)[None, :]).astype(
        jnp.int32
    )
    rank_of = jnp.sum((jnp.cumsum(onehot, axis=0) - 1) * onehot, axis=1)
    slot_of = flat_routes * capacity + rank_of
    source_of = (
        jnp.zeros((EXPERTS * capacity,), jnp.int32)
        .at[slot_of]
        .set(jnp.arange(token_count * top_count, dtype=jnp.int32))
    )

    def arrange(slots, width):
        blocks = slots.reshape(EXPERTS, capacity, width)
        if copies > 1:
            return jnp.repeat(blocks, copies, axis=0)
        return blocks.reshape(expert_count, hosted * capacity, width)

    def own_of(arrived):
        own_rows = lax.dynamic_slice_in_dim(arrived, offset, capacity, 1)
        return own_rows.reshape(expert_count * capacity, feature_width)

    def send_out(slots):
        blocks = arrange(slots, feature_width)
        arrived = lax.all_to_all(blocks, "expert", split_axis=0, concat_axis=0, tiled=True)
        return own_of(arrived)

    token_slots = jnp.take(tokens[0], source_of // top_count, axis=0)
    features = send_out(token_slots)
    columns = feature_width // client_count
    row_total = features.shape[0]
    pieces = features.reshape(row_total, client_count, columns)
    foreign = lax.all_to_all(pieces, "client", split_axis=1, concat_axis=1, tiled=True)
    gate_parts = jnp.einsum("rcw,uw->cru", foreign, gate_proj, preferred_element_type=jnp.float32)
    up_parts = jnp.einsum("rcw,uw->cru", foreign, up_proj, preferred_element_type=jnp.float32)
    gate_back, up_back = (
        lax.all_to_all(
            gate_parts.astype(jnp.bfloat16), "client", split_axis=0, concat_axis=0, tiled=True
        ).astype(gate_parts.dtype),
        lax.all_to_all(
            up_parts.astype(jnp.bfloat16), "client", split_axis=0, concat_axis=0, tiled=True
        ).astype(up_parts.dtype),
    )
    gate_pre = jnp.sum(gate_back, axis=0)
    up_pre = jnp.sum(up_back, axis=0)
    hidden = (jax.nn.silu(gate_pre) * up_pre).astype(jnp.bfloat16)
    down_full = lax.all_gather(down_proj, "client", axis=1, tiled=True)
    control = correction[0]
    grad_sum = None
    gate_rows = gate_weights[0]
    positions = expert_index * token_count + jnp.arange(token_count, dtype=jnp.int32)
    live_rows = (positions < counts[client_index]).astype(jnp.float32)
    sender_expert = (
        (jnp.arange(expert_count, dtype=jnp.int32) * shard_count + shard_index) * unit_count // FF
    )
    select = (jnp.arange(EXPERTS, dtype=jnp.int32)[:, None] == sender_expert[None, :]).astype(
        jnp.bfloat16
    )
    target_rows = target[0].astype(jnp.float32)
    step_size = 2.0 / FF
    for step_number in range(LOCAL_STEPS):
        if step_number == 0:
            current = down_full
        else:
            current = (
                down_full.astype(jnp.float32)
                - step_size * (grad_sum + float(step_number) * control.astype(jnp.float32))
            ).astype(jnp.bfloat16)
        partial_value = jnp.dot(hidden, current, preferred_element_type=jnp.float32).astype(
            jnp.bfloat16
        )
        returned = lax.all_to_all(
            partial_value.reshape(expert_count, capacity, feature_width),
            "expert",
            split_axis=0,
            concat_axis=0,
            tiled=True,
        )
        slot_sums = jnp.einsum("ej,jcd->ecd", select, returned, preferred_element_type=jnp.float32)
        slot_sums = slot_sums.reshape(EXPERTS * capacity, feature_width)
        picked = jnp.take(slot_sums, slot_of, axis=0).reshape(token_count, top_count, feature_width)
        plane_rows = jnp.sum(gate_rows[:, :, None] * picked, axis=1)
        output = lax.psum(plane_rows.astype(jnp.bfloat16), "shard").astype(jnp.float32)
        residual = live_rows[:, None] * (output - target_rows)
        cotangent = (gate_rows[:, :, None] * residual[:, None, :]).astype(jnp.bfloat16)
        cotangent = cotangent.reshape(token_count * top_count, feature_width)
        arrived = send_out(jnp.take(cotangent, source_of, axis=0))
        gradient = lax.dot_general(
            hidden, arrived, (((0,), (0,)), ((), ())), preferred_element_type=jnp.float32
        )
        if step_number == 0:
            grad_sum = gradient
        else:
            grad_sum = grad_sum + gradient
    weight_share = counts[client_index].astype(jnp.float32) / jnp.sum(counts).astype(jnp.float32)
    client_term = (weight_share * (grad_sum / LOCAL_STEPS + control.astype(jnp.float32))).astype(
        jnp.bfloat16
    )
    client_term = client_term.reshape(unit_count, client_count, feature_width // client_count)
    received = lax.all_to_all(client_term, "client", split_axis=1, concat_axis=1, tiled=True)
    return jnp.sum(received.astype(jnp.float32), axis=1)


def solution(mesh):
    return jax.shard_map(
        local,
        mesh=mesh,
        in_specs=(
            P("client", "expert", None),
            P("client", "expert", None),
            P("client", "expert", None),
            P("client", "expert", None),
            P(),
            P(("expert", "shard"), "client"),
            P(("expert", "shard"), "client"),
            P(("expert", "shard"), "client"),
            P("client", ("expert", "shard"), None),
        ),
        out_specs=P(("expert", "shard"), "client"),
        check_vma=False,
    )
```

profile of v0, /device:TPU:0, one launch (start us, length us, event | category | flops | bytes accessed | tf_op | source)
XLA Modules:
  0.0 1802.7 jit_solution(7563019021843828559)
XLA Ops:
  6.5 10.0 copy.33
  18.9 1.4 scatter_custom_fusion
  20.4 1.4 gather_fusion
  22.9 5.2 all-to-all-start
  28.1 13.6 all-to-all-done
  42.2 34.4 %all_to_all.45 = bf16[128,4,512]{2,0,1:T(8,128)(2,1)S(1)} all-to-all(bf16[128,4,512]{2,0,1:T(8,128)(2,1)S(1)} %copy.30), channel_id=1, replica_groups=mesh['client'=4,'expert'=4,'shard'=2] {'client'}, dimensions={1} | all-to-all | bytes 1048576 | tf_op jit(solution)/shard_map/all_to_all | solution.py:61
  76.6 9.1 fusion.8
  85.7 5.4 all-to-all-start.3
  91.2 9.2 fusion.7
  100.4 361.1 %all-to-all-done.3 = bf16[4,128,7168]{2,1,0:T(8,128)(2,1)} async-done(((bf16[4,128,7168]{2,1,0:T(8,128)(2,1)}), bf16[4,128,7168]{2,1,0:T(8,128)(2,1)}, u32[]{:S(2)}, u32[]{:S(2)}) %all-to-all-start.3) | async-done | bytes 7340064 | tf_op jit(solution)/shard_map/all_to_all | solution.py:68
  461.5 5.7 all-to-all-start.2
  467.3 6.7 convert_reduce_fusion.1
  474.0 312.4 %all-to-all-done.2 = bf16[4,128,7168]{2,1,0:T(8,128)(2,1)} async-done(((bf16[4,128,7168]{2,1,0:T(8,128)(2,1)}), bf16[4,128,7168]{2,1,0:T(8,128)(2,1)}, u32[]{:S(2)}, u32[]{:S(2)}) %all-to-all-start.2) | async-done | bytes 7340064 | tf_op jit(solution)/shard_map/all_to_all | solution.py:65
  786.3 5.0 convert_reduce_fusion.2
  792.3 45.8 %all-gather.2.cloned.1.call-done = bf16[7168,2048]{0,1:T(8,128)(2,1)} async-done(((bf16[7168,512]{0,1:T(8,128)(2,1)}), bf16[7168,2048]{0,1:T(8,128)(2,1)}) %all-gather.2.cloned.1.call-update) | async-done | bytes 29360144 | tf_op jit(solution)/shard_map/all_gather | solution.py:75
  838.1 15.6 convolution_convert_fusion.2
  853.7 3.6 all-to-all-start.4
  858.0 7.6 all-to-all-done.4
  866.3 1.2 copy.35
  867.5 2.7 gather_fusion.1
  870.2 1.8 broadcast_select_fusion.1
  872.0 2.2 reshape.133
  874.3 5.6 multiply_reduce_fusion.1
  881.4 14.4 all-reduce.3.cloned.1.call-done
  895.9 1.2 fusion.14
  898.3 2.4 mul.157
  900.7 1.8 multiply_convert_fusion.2
  902.5 1.4 gather_fusion.2
  905.0 3.9 all-to-all-start.5
  909.1 35.2 %copy.36 = bf16[1,7168,2048]{1,2,0:T(8,128)(2,1)} copy(bf16[1,7168,2048]{2,1,0:T(8,128)(2,1)} %param.21) | data formatting | bytes 58720256 | tf_op args[8]
  944.3 22.5 %fusion.30 = f32[7168,2048]{0,1:T(8,128)} fusion(bf16[128,7168]{1,0:T(8,128)(2,1)S(1)} %copy-done.3, bf16[128,2048]{1,0:T(8,128)(2,1)S(1)} %bitcast.63), kind=kOutput, calls=%fused_computation.76 | convolution fusion | flops 3758096384 | bytes 61079552 | tf_op jit(solution)/shard_map/dot_general | solution.py:116
  966.9 37.3 %fusion.11 = bf16[128,2048]{1,0:T(8,128)(2,1)S(1)} fusion(bf16[128,7168]{1,0:T(8,128)(2,1)S(1)} %copy-done.3, f32[7168,2048]{0,1:T(8,128)} %fusion.30, bf16[7168,2048]{0,1:T(8,128)(2,1)} %all-gather.2.cloned.1.call-done, bf16[1,7168,2048]{1,2,0:T(8,128)(2,1)} %copy.36), kind=kOutput, calls=%fused_computation.24 | convolution fusion | flops 3846438912 | bytes 119799808 | tf_op jit(solution)/shard_map/dot_general | solution.py:97
  1004.2 12.4 all_to_all.46
  1017.3 1.2 copy.38
  1018.5 2.7 gather_fusion.3
  1021.2 1.8 broadcast_select_fusion
  1023.0 2.2 reshape.137
  1025.2 5.6 multiply_reduce_fusion
  1030.8 18.3 %all-reduce.5.cloned.1.call-done = bf16[128,2048]{1,0:T(8,128)(2,1)} async-done(((bf16[128,2048]{1,0:T(8,128)(2,1)}), bf16[128,2048]{1,0:T(8,128)(2,1)}) %all-reduce.5.cloned.1.call-update) | async-done | bytes 524304 | tf_op jit(solution)/shard_map/psum | solution.py:111
  1051.6 2.4 mul.164
  1054.0 1.8 multiply_convert_fusion.1
  1055.8 1.4 gather_fusion.4
  1058.3 3.9 all-to-all-start.7
  1064.3 12.0 all-to-all-done.7
  1076.3 39.4 %fusion.4 = bf16[7168,2048]{0,1:T(8,128)(2,1)} fusion(f32[7168,2048]{0,1:T(8,128)} %fusion.30, bf16[1,7168,2048]{1,2,0:T(8,128)(2,1)} %copy.36, f32[]{:T(128)S(6)} %div.40, bf16[128,7168]{1,0:T(8,128)(2,1)S(1)} %copy-done.4, bf16[128,2048]{1,0:T(8,128)(2,1)S(1)} %bitcast.62), kind=kOutput, calls=%fused_computation.12 | convolution fusion | flops 3846176768 | bytes 119799808 | tf_op jit(solution)/shard_map/dot_general | solution.py:116
  1115.8 648.5 %all_to_all.47 = bf16[7168,4,512]{0,2,1:T(8,128)(2,1)} all-to-all(bf16[7168,4,512]{0,2,1:T(8,128)(2,1)} %bitcast.59), channel_id=1, replica_groups=mesh['client'=4,'expert'=4,'shard'=2] {'client'}, dimensions={1} | all-to-all | bytes 58720256 | tf_op jit(solution)/shard_map/all_to_all | solution.py:128
  1764.2 16.4 convert_reduce_fusion
  1780.6 15.3 copy.39
  (70 shorter events, 15.2 us)
Async XLA Ops:
  6.5 13.9 copy-start
  6.5 831.6 %all-gather.2.cloned.1.call-start = ((), (), s32[]{:S(2)}) async-start(), calls=%async_computation.9 | async-start | bytes 36700160 | tf_op jit(solution)/shard_map/all_gather | solution.py:75
  16.6 0.7 copy-start.9
  22.9 18.8 %all-to-all-start = ((bf16[4,64,2048]{2,1,0:T(8,128)(2,1)}), bf16[4,64,2048]{2,1,0:T(8,128)(2,1)S(1)}, u32[]{:S(2)}, u32[]{:S(2)}) async-start(bf16[4,64,2048]{2,1,0:T(8,128)(2,1)} %broadcast_select_fusion.4), calls=%async_computation | async-start | bytes 2097152 | tf_op jit(solution)/shard_map/all_to_all | solution.py:53
  85.7 375.8 %all-to-all-start.3 = ((bf16[4,128,7168]{2,1,0:T(8,128)(2,1)}), bf16[4,128,7168]{2,1,0:T(8,128)(2,1)}, u32[]{:S(2)}, u32[]{:S(2)}) async-start(bf16[4,128,7168]{2,1,0:T(8,128)(2,1)} %fusion.8), calls=%async_computation.3 | async-start | bytes 14680064 | tf_op jit(solution)/shard_map/all_to_all | solution.py:68
  461.5 324.8 %all-to-all-start.2 = ((bf16[4,128,7168]{2,1,0:T(8,128)(2,1)}), bf16[4,128,7168]{2,1,0:T(8,128)(2,1)}, u32[]{:S(2)}, u32[]{:S(2)}) async-start(bf16[4,128,7168]{2,1,0:T(8,128)(2,1)} %fusion.7), calls=%async_computation.2 | async-start | bytes 14680064 | tf_op jit(solution)/shard_map/all_to_all | solution.py:65
  786.3 5.0 copy-start.5
  792.3 61.4 %copy-start.2 = (bf16[128,7168]{1,0:T(8,128)(2,1)}, bf16[128,7168]{1,0:T(8,128)(2,1)S(1)}, u32[]{:S(2)}) copy-start(bf16[128,7168]{1,0:T(8,128)(2,1)S(1)} %multiply_convert_fusion) | copy-start | bytes 5505028
  792.3 65.5 %copy-start.8 = (f32[1,128,2]{1,2,0:T(2,128)S(1)}, f32[1,128,2]{1,2,0:T(2,128)}, u32[]{:S(2)}) copy-start(f32[1,128,2]{1,2,0:T(2,128)} %param.16) | copy-start | bytes 3076
  853.7 11.9 all-to-all-start.4
  857.4 38.5 %all-reduce.3.cloned.1.call-start = ((), (), s32[]{:S(2)}) async-start(), calls=%async_computation.10 | async-start | bytes 1048576 | tf_op jit(solution)/shard_map/psum | solution.py:111
  872.0 8.1 copy-start.10
  872.0 23.9 %copy-start.6 = (bf16[1,128,2048]{2,1,0:T(8,128)(2,1)S(1)}, bf16[1,128,2048]{2,1,0:T(8,128)(2,1)}, u32[]{:S(2)}) copy-start(bf16[1,128,2048]{2,1,0:T(8,128)(2,1)} %param.14) | copy-start | bytes 1572868
  905.0 39.3 %all-to-all-start.5 = ((bf16[4,64,2048]{2,1,0:T(8,128)(2,1)}), bf16[4,64,2048]{2,1,0:T(8,128)(2,1)S(1)}, u32[]{:S(2)}, u32[]{:S(2)}) async-start(bf16[4,64,2048]{2,1,0:T(8,128)(2,1)} %bitcast.16), calls=%async_computation.5 | async-start | bytes 2097152 | tf_op jit(solution)/shard_map/all_to_all | solution.py:53
  908.9 35.4 %copy-start.3 = (bf16[128,7168]{1,0:T(8,128)(2,1)S(1)}, bf16[128,7168]{1,0:T(8,128)(2,1)}, u32[]{:S(2)}) copy-start(bf16[128,7168]{1,0:T(8,128)(2,1)} %copy-done.2) | copy-start | bytes 5505028
  908.9 140.2 %all-reduce.5.cloned.1.call-start = ((), (), s32[]{:S(2)}) async-start(), calls=%async_computation.11 | async-start | bytes 1048576 | tf_op jit(solution)/shard_map/psum | solution.py:111
  1023.0 26.2 %copy-start.7 = (bf16[1,128,2048]{2,1,0:T(8,128)(2,1)S(1)}, bf16[1,128,2048]{2,1,0:T(8,128)(2,1)}, u32[]{:S(2)}) copy-start(bf16[1,128,2048]{2,1,0:T(8,128)(2,1)} %param.14) | copy-start | bytes 1572868
  1057.1 19.2 %copy-start.4 = (bf16[128,7168]{1,0:T(8,128)(2,1)S(1)}, bf16[128,7168]{1,0:T(8,128)(2,1)}, u32[]{:S(2)}) copy-start(bf16[128,7168]{1,0:T(8,128)(2,1)} %copy-done.2) | copy-start | bytes 5505028
  1058.3 18.0 all-to-all-start.7
  1780.6 15.4 copy-start.1
Sparse Core Ops, SparseCore 0:
  16.7 821.3 all-gather.1
  880.0 15.8 all-reduce.2
  1031.0 18.1 all-reduce.4
where the time goes:
time: 1810 us; the launch traced here: 1800 us
  waiting for transfers between devices  785 us (43%)
  blocking collectives  695 us (38%)
  matrix products  135 us (7%)
  local copies, waits for them, and re-layouts  88.8 us (5%)
  other arithmetic  55.3 us (3%)
  starting transfers between devices  28.5 us (2%)
    all_to_all x1, blocking collectives, local(): lax.all_to_all(client_term, 'client', split_axis=1, concat_axis=1, tiled=...  648 us
    all_to_all x1, waiting for transfers between devices, local(): lax.all_to_all(up_parts.astype(jnp.bfloat16), 'client', split_axis=0, con...  361 us
    all_to_all x1, waiting for transfers between devices, local(): lax.all_to_all(gate_parts.astype(jnp.bfloat16), 'client', split_axis=0, c...  312 us
    dot_general x2, matrix products, local(): lax.dot_general(hidden, arrived, (((0,), (0,)), ((), ())), preferred_elem...  61.9 us
    dot_general x2, matrix products, local(): jnp.dot(hidden, current, preferred_element_type=jnp.float32)  53 us
    unnamed x26, local copies, waits for them, and re-layouts  46.1 us
    all_gather x1, waiting for transfers between devices, local(): down_full = lax.all_gather(down_proj, 'client', axis=1, tiled=True)  45.8 us
  transfers between devices with their start and end apart: 9, of which 8 were waited for; matrix products, arithmetic and copies ran while one was open for 4% of the time, Pallas kernels for 0%

commit v1 on v0

--- a/solution.py
+++ b/solution.py
@@ -6,6 +6,16 @@
 FF = 7168
 EXPERTS = 8
 LOCAL_STEPS = 2
+
+
+def gather_line(own, count):
+    ahead, behind = [own], [own]
+    for step in range(1, count):
+        up = [(j, j + 1) for j in range(step - 1, count - 1)]
+        down = [(j + 1, j) for j in range(0, count - step)]
+        behind.append(lax.ppermute(behind[-1], "client", up))
+        ahead.append(lax.ppermute(ahead[-1], "client", down))
+    return [own] + [ahead[k] + behind[count - k] for k in range(1, count)]
 
 
 def local(tokens, target, routes, gate_weights, counts, gate_proj, up_proj, down_proj, correction):
@@ -26,6 +36,10 @@
     own_expert = (expert_index * shard_count + shard_index) * unit_count // FF
     first_expert = expert_index * per_index // FF
     offset = (own_expert - first_expert) * capacity
+    weight_share = counts[client_index].astype(jnp.float32) / jnp.sum(counts).astype(jnp.float32)
+    control = correction[0]
+    scaled = (weight_share * control.astype(jnp.float32)).astype(jnp.bfloat16)
+    control_sum = lax.psum_scatter(scaled, "client", scatter_dimension=1, tiled=True)
     flat_routes = routes[0].reshape(-1)
     onehot = (flat_routes[:, None] == jnp.arange(EXPERTS, dtype=jnp.int32)[None, :]).astype(
         jnp.int32
@@ -72,61 +86,88 @@
     gate_pre = jnp.sum(gate_back, axis=0)
     up_pre = jnp.sum(up_back, axis=0)
     hidden = (jax.nn.silu(gate_pre) * up_pre).astype(jnp.bfloat16)
-    down_full = lax.all_gather(down_proj, "client", axis=1, tiled=True)
-    control = correction[0]
-    grad_sum = None
+    gathered = gather_line(hidden, client_count)
+    spread = jnp.concatenate(gathered, axis=0)
+    order = (client_index + jnp.arange(client_count, dtype=jnp.int32)) % client_count
+    inverse = (jnp.arange(client_count, dtype=jnp.int32) - client_index) % client_count
+    by_slot = jnp.dot(spread, down_proj, preferred_element_type=jnp.float32).astype(jnp.bfloat16)
+    by_client = jnp.take(by_slot.reshape(client_count, row_total, columns), inverse, axis=0)
+    first_piece = lax.all_to_all(by_client, "client", split_axis=0, concat_axis=0, tiled=True)
+    first_piece = jnp.swapaxes(first_piece, 0, 1).reshape(row_total, feature_width)
+    overlap = lax.dot_general(
+        hidden, hidden, (((1,), (1,)), ((), ())), preferred_element_type=jnp.float32
+    )
+    overlap_high = overlap.astype(jnp.bfloat16)
+    overlap_low = (overlap - overlap_high.astype(jnp.float32)).astype(jnp.bfloat16)
+    overlap_pair = jnp.concatenate([overlap_high, overlap_low], axis=1)
+    shift_piece = jnp.dot(hidden, control, preferred_element_type=jnp.float32)
     gate_rows = gate_weights[0]
     positions = expert_index * token_count + jnp.arange(token_count, dtype=jnp.int32)
     live_rows = (positions < counts[client_index]).astype(jnp.float32)
     sender_expert = (
         (jnp.arange(expert_count, dtype=jnp.int32) * shard_count + shard_index) * unit_count // FF
     )
-    select = (jnp.arange(EXPERTS, dtype=jnp.int32)[:, None] == sender_expert[None, :]).astype(
-        jnp.bfloat16
+    flat_gates = gate_rows.reshape(-1)
+    sender_slot = sender_expert[:, None] * capacity + jnp.arange(capacity, dtype=jnp.int32)[None, :]
+    sender_slot = sender_slot.reshape(-1)
+    by_choice = slot_of.reshape(token_count, top_count)
+    combine = jnp.sum(
+        jnp.where(
+            by_choice[:, :, None] == sender_slot[None, None, :], gate_rows[:, :, None], 0.0
+        ),
+        axis=1,
     )
+    combine_high = combine.astype(jnp.bfloat16)
+    combine_low = (combine - combine_high.astype(jnp.float32)).astype(jnp.bfloat16)
+    combine_pair = jnp.concatenate([combine_high, combine_low], axis=1)
+    slot_gates = jnp.take(flat_gates, source_of, axis=0)
+    slot_tokens = source_of // top_count
     target_rows = target[0].astype(jnp.float32)
     step_size = 2.0 / FF
+    cotangents = []
     for step_number in range(LOCAL_STEPS):
         if step_number == 0:
-            current = down_full
+            partial_value = first_piece
         else:
-            current = (
-                down_full.astype(jnp.float32)
-                - step_size * (grad_sum + float(step_number) * control.astype(jnp.float32))
+            moved = sum(cotangents[1:], cotangents[0].astype(jnp.float32))
+            moved = moved.astype(jnp.bfloat16)
+            drift = jnp.dot(
+                overlap_pair,
+                jnp.concatenate([moved, moved], axis=0),
+                preferred_element_type=jnp.float32,
+            )
+            partial_value = (
+                first_piece.astype(jnp.float32)
+                - step_size * (drift + float(step_number) * shift_piece)
             ).astype(jnp.bfloat16)
-        partial_value = jnp.dot(hidden, current, preferred_element_type=jnp.float32).astype(
-            jnp.bfloat16
-        )
         returned = lax.all_to_all(
             partial_value.reshape(expert_count, capacity, feature_width),
             "expert",
             split_axis=0,
             concat_axis=0,
             tiled=True,
-        )
-        slot_sums = jnp.einsum("ej,jcd->ecd", select, returned, preferred_element_type=jnp.float32)
-        slot_sums = slot_sums.reshape(EXPERTS * capacity, feature_width)
-        picked = jnp.take(slot_sums, slot_of, axis=0).reshape(token_count, top_count, feature_width)
-        plane_rows = jnp.sum(gate_rows[:, :, None] * picked, axis=1)
-        output = lax.psum(plane_rows.astype(jnp.bfloat16), "shard").astype(jnp.float32)
+        ).reshape(expert_count * capacity, feature_width)
+        plane_rows = jnp.dot(
+            combine_pair,
+            jnp.concatenate([returned, returned], axis=0),
+            preferred_element_type=jnp.float32,
+        ).astype(jnp.bfloat16)
+        output = plane_rows.astype(jnp.float32)
+        for turn in range(1, shard_count):
+            ring = [(j, (j + turn) % shard_count) for j in range(shard_count)]
+            output = output + lax.ppermute(plane_rows, "shard", ring).astype(jnp.float32)
         residual = live_rows[:, None] * (output - target_rows)
-        cotangent = (gate_rows[:, :, None] * residual[:, None, :]).astype(jnp.bfloat16)
-        cotangent = cotangent.reshape(token_count * top_count, feature_width)
-        arrived = send_out(jnp.take(cotangent, source_of, axis=0))
-        gradient = lax.dot_general(
-            hidden, arrived, (((0,), (0,)), ((), ())), preferred_element_type=jnp.float32
-        )
-        if step_number == 0:
-            grad_sum = gradient
-        else:
-            grad_sum = grad_sum + gradient
-    weight_share = counts[client_index].astype(jnp.float32) / jnp.sum(counts).astype(jnp.float32)
-    client_term = (weight_share * (grad_sum / LOCAL_STEPS + control.astype(jnp.float32))).astype(
-        jnp.bfloat16
+        cotangent = slot_gates[:, None] * jnp.take(residual, slot_tokens, axis=0)
+        cotangents.append(send_out(cotangent.astype(jnp.bfloat16)))
+    mean_rows = sum(c.astype(jnp.float32) for c in cotangents)
+    mean_rows = (mean_rows * (weight_share / LOCAL_STEPS)).astype(jnp.bfloat16)
+    mean_rows = jnp.swapaxes(mean_rows.reshape(row_total, client_count, columns), 0, 1)
+    mean_rows = lax.all_to_all(mean_rows, "client", split_axis=0, concat_axis=0, tiled=True)
+    mean_rows = jnp.take(mean_rows, order, axis=0).reshape(client_count * row_total, columns)
+    gradient = lax.dot_general(
+        spread, mean_rows, (((0,), (0,)), ((), ())), preferred_element_type=jnp.float32
     )
-    client_term = client_term.reshape(unit_count, client_count, feature_width // client_count)
-    received = lax.all_to_all(client_term, "client", split_axis=1, concat_axis=1, tiled=True)
-    return jnp.sum(received.astype(jnp.float32), axis=1)
+    return gradient + control_sum.astype(jnp.float32)
 
 
 def solution(mesh):

time: 1810 us -> 1110 us (0.61)
  blocking collectives: 695 us -> 45.7 us
  waiting for transfers between devices: 785 us -> 881 us
  matrix products: 135 us -> 51 us
  local copies, waits for them, and re-layouts: 88.8 us -> 21.6 us
  starting transfers between devices: 28.5 us -> 48 us
    all_to_all x1 -> x0, blocking collectives: 648 us -> none  [local(): lax.all_to_all(client_term, 'client', split_axis=1, concat_axis=1, tiled=...]
    ppermute x0 -> x8, waiting for transfers between devices: none -> 173 us  [the longest x3 171 us: gather_line(): ahead.append(lax.ppermute(ahead[-1], 'client', down))]
    dot_general x6 -> x7, matrix products: 116 us -> 32.6 us  [the longest x1 11.4 us: local(): shift_piece = jnp.dot(hidden, control, preferred_element_type=jnp.float32)]
    all_gather x1 -> x0, waiting for transfers between devices: 45.8 us -> none  [local(): down_full = lax.all_gather(down_proj, 'client', axis=1, tiled=True)]
    unnamed x26, local copies, waits for them, and re-layouts: 46.1 us -> 1.31 us
    psum x2 -> x0, waiting for transfers between devices: 32.7 us -> none  [local(): lax.psum(plane_rows.astype(jnp.bfloat16), 'shard').astype(jnp.float32)]
    reduce_sum x3 -> x1, other arithmetic: 27.6 us -> 0.15 us  [local(): jnp.sum(jnp.where(by_choice[:, :, None] == sender_slot[None, None, :], ga...]
    all_to_all x0 -> x2, waiting for transfers between devices: none -> 26.9 us  [the longest x1 14.1 us: local(): lax.all_to_all(mean_rows, 'client', split_axis=0, concat_axis=0, tiled=True)]
  transfers between devices with their start and end apart: 9 -> 17, of which waited for: 8 -> 12; matrix products, arithmetic and copies ran while one was open for 4% -> 8% of each run, Pallas kernels for 0% -> 0%
where the time goes in v1:
time: 1110 us
  waiting for transfers between devices  881 us (79%)
  matrix products  51 us (5%)
  other arithmetic  49.1 us (4%)
  starting transfers between devices  48 us (4%)
  blocking collectives  45.7 us (4%)
  local copies, waits for them, and re-layouts  21.6 us (2%)
  between operations  15.3 us (1%)
    all_to_all x1, waiting for transfers between devices, local(): lax.all_to_all(up_parts.astype(jnp.bfloat16), 'client', split_axis=0, con...  336 us
    all_to_all x1, waiting for transfers between devices, local(): lax.all_to_all(gate_parts.astype(jnp.bfloat16), 'client', split_axis=0, c...  310 us
    ppermute x3, waiting for transfers between devices, gather_line(): ahead.append(lax.ppermute(ahead[-1], 'client', down))  171 us
    all_to_all x1, blocking collectives, local(): lax.all_to_all(pieces, 'client', split_axis=1, concat_axis=1, tiled=True)  33.8 us
    all_to_all x3, waiting for transfers between devices, send_out(): lax.all_to_all(blocks, 'expert', split_axis=0, concat_axis=0, tiled=True)  28.7 us
  transfers between devices with their start and end apart: 17, of which 12 were waited for; matrix products, arithmetic and copies ran while one was open for 8% of the time, Pallas kernels for 0%

profile of v1, /device:TPU:0, one launch (start us, length us, event | category | flops | bytes accessed | tf_op | source)
XLA Modules:
  0.0 1111.8 jit_solution(4470953247502673579)
XLA Ops:
  6.5 1.3 reduce_sum.55
  7.9 1.3 dynamic_slice.14
  10.5 20.4 %multiply_convert_fusion = bf16[7168,2048]{1,0:T(8,128)(2,1)} fusion(bf16[1,7168,2048]{2,1,0:T(8,128)(2,1)} %param.21, f32[]{:T(128)S(6)} %div.46), kind=kLoop, calls=%fused_computation.7 | loop fusion | flops 44040192 | bytes 58720260 | tf_op jit(solution)/shard_map/convert_element_type | solution.py:41
  33.1 1.4 scatter_custom_fusion
  34.6 1.4 gather_fusion
  37.1 5.2 all-to-all-start
  42.3 13.6 %all-to-all-done = bf16[4,64,2048]{2,1,0:T(8,128)(2,1)S(1)} async-done(((bf16[4,64,2048]{2,1,0:T(8,128)(2,1)}), bf16[4,64,2048]{2,1,0:T(8,128)(2,1)S(1)}, u32[]{:S(2)}, u32[]{:S(2)}) %all-to-all-start) | async-done | bytes 1048608 | tf_op jit(solution)/shard_map/all_to_all | solution.py:67
  56.4 33.8 %all_to_all.50 = bf16[128,4,512]{2,0,1:T(8,128)(2,1)S(1)} all-to-all(bf16[128,4,512]{2,0,1:T(8,128)(2,1)S(1)} %copy.31), channel_id=1, replica_groups=mesh['client'=4,'expert'=4,'shard'=2] {'client'}, dimensions={1} | all-to-all | bytes 1048576 | tf_op jit(solution)/shard_map/all_to_all | solution.py:75
  90.2 9.1 fusion.3
  99.4 5.4 all-to-all-start.3
  104.8 9.2 fusion.2
  114.0 336.3 %all-to-all-done.3 = bf16[4,128,7168]{2,1,0:T(8,128)(2,1)} async-done(((bf16[4,128,7168]{2,1,0:T(8,128)(2,1)}), bf16[4,128,7168]{2,1,0:T(8,128)(2,1)}, u32[]{:S(2)}, u32[]{:S(2)}) %all-to-all-start.3) | async-done | bytes 7340064 | tf_op jit(solution)/shard_map/all_to_all | solution.py:82
  450.3 5.7 all-to-all-start.2
  456.1 6.6 convert_reduce_fusion
  462.6 310.0 %all-to-all-done.2 = bf16[4,128,7168]{2,1,0:T(8,128)(2,1)} async-done(((bf16[4,128,7168]{2,1,0:T(8,128)(2,1)}), bf16[4,128,7168]{2,1,0:T(8,128)(2,1)}, u32[]{:S(2)}, u32[]{:S(2)}) %all-to-all-start.2) | async-done | bytes 7340064 | tf_op jit(solution)/shard_map/all_to_all | solution.py:79
  772.7 5.0 convert_reduce_fusion.1
  778.6 1.3 collective-permute-start
  779.9 4.7 collective-permute-start.1
  784.6 85.0 %collective-permute-done = bf16[128,7168]{1,0:T(8,128)(2,1)S(1)} collective-permute-done((bf16[128,7168]{1,0:T(8,128)(2,1)S(1)}, bf16[128,7168]{1,0:T(8,128)(2,1)S(1)}, u32[]{:S(2)}, u32[]{:S(2)}) %collective-permute-start) | collective-permute-done | bytes 1835040 | tf_op jit(solution)/shard_map/ppermute | solution.py:17
  869.6 1.3 collective-permute-start.4
  871.7 44.8 %collective-permute-done.4 = bf16[128,7168]{1,0:T(8,128)(2,1)S(1)} collective-permute-done((bf16[128,7168]{1,0:T(8,128)(2,1)S(1)}, bf16[128,7168]{1,0:T(8,128)(2,1)S(1)}, u32[]{:S(2)}, u32[]{:S(2)}) %collective-permute-start.4) | collective-permute-done | bytes 1835040 | tf_op jit(solution)/shard_map/ppermute | solution.py:17
  916.5 1.3 collective-permute-start.5
  919.1 41.4 %collective-permute-done.5 = bf16[128,7168]{1,0:T(8,128)(2,1)S(1)} collective-permute-done((bf16[128,7168]{1,0:T(8,128)(2,1)S(1)}, bf16[128,7168]{1,0:T(8,128)(2,1)S(1)}, u32[]{:S(2)}, u32[]{:S(2)}) %collective-permute-start.5) | collective-permute-done | bytes 1835040 | tf_op jit(solution)/shard_map/ppermute | solution.py:17
  961.4 7.8 convolution_convert_fusion.4
  970.8 6.5 all-to-all-start.4
  977.5 12.7 %all-to-all-done.4 = bf16[4,128,512]{2,1,0:T(8,128)(2,1)S(1)} async-done(((bf16[4,128,512]{2,1,0:T(8,128)(2,1)}), bf16[4,128,512]{2,1,0:T(8,128)(2,1)S(1)}, u32[]{:S(2)}, u32[]{:S(2)}) %all-to-all-start.4) | async-done | bytes 524320 | tf_op jit(solution)/shard_map/all_to_all | solution.py:95
  990.6 1.2 reshape_reshape.14
  991.8 3.7 all-to-all-start.5
  995.9 6.1 all-to-all-done.5
  1002.6 1.9 gather_fusion.1
  1005.3 1.6 fusion.11
  1006.9 2.7 gather_fusion.3
  1009.6 2.9 fusion.10
  1012.4 4.2 all-to-all-start.6
  1016.7 11.4 %fusion = f32[128,2048]{1,0:T(8,128)S(1)} fusion(bf16[128,7168]{1,0:T(8,128)(2,1)S(1)} %multiply_convert_fusion.1, bf16[1,7168,2048]{2,1,0:T(8,128)(2,1)} %param.21), kind=kOutput, calls=%fused_computation.8 | convolution fusion | flops 3758096384 | bytes 32243712 | tf_op jit(solution)/shard_map/dot_general | solution.py:103
  1031.3 1.1 constant_dynamic-slice_fusion
  1032.5 1.6 fusion.8
  1034.0 11.9 %all_to_all.51 = bf16[4,32,2048]{2,1,0:T(8,128)(2,1)S(1)} all-to-all(bf16[4,32,2048]{2,1,0:T(8,128)(2,1)S(1)} %bitcast.59), channel_id=1, replica_groups=mesh['client'=4,'expert'=4,'shard'=2] {'expert'}, dimensions={0} | all-to-all | bytes 1048576 | tf_op jit(solution)/shard_map/all_to_all | solution.py:143
  1046.3 1.9 collective-permute-done.7
  1048.5 2.7 gather_fusion.4
  1051.2 2.9 fusion.9
  1054.0 3.5 all-to-all-start.8
  1057.5 14.2 %all-to-all-done.8 = bf16[4,64,2048]{2,1,0:T(8,128)(2,1)S(1)} async-done(((bf16[4,64,2048]{2,1,0:T(8,128)(2,1)}), bf16[4,64,2048]{2,1,0:T(8,128)(2,1)S(1)}, u32[]{:S(2)}, u32[]{:S(2)}) %all-to-all-start.8) | async-done | bytes 1048608 | tf_op jit(solution)/shard_map/all_to_all | solution.py:67
  1071.7 2.0 multiply_convert_fusion.2
  1073.7 1.4 convert_element_type.161
  1076.0 3.5 all-to-all-start.9
  1079.6 14.1 %all-to-all-done.9 = bf16[4,128,512]{2,1,0:T(8,128)(2,1)S(1)} async-done(((bf16[4,128,512]{2,1,0:T(8,128)(2,1)}), bf16[4,128,512]{2,1,0:T(8,128)(2,1)S(1)}, u32[]{:S(2)}, u32[]{:S(2)}) %all-to-all-start.9) | async-done | bytes 524320 | tf_op jit(solution)/shard_map/all_to_all | solution.py:165
  1094.4 10.5 convert_add_fusion
  (92 shorter events, 16.9 us)
Async XLA Ops:
  6.5 28.1 %copy-start = (bf16[1,128,2048]{2,1,0:T(8,128)(2,1)S(1)}, bf16[1,128,2048]{2,1,0:T(8,128)(2,1)}, u32[]{:S(2)}) copy-start(bf16[1,128,2048]{2,1,0:T(8,128)(2,1)} %param.13) | copy-start | bytes 1572868
  6.5 1087.9 %reduce-scatter.2.cloned.1.call-start = ((), (), s32[]{:S(2)}) async-start(), calls=%async_computation.11 | async-start | bytes 36700160 | tf_op jit(solution)/shard_map/reduce_scatter | solution.py:42
  30.9 0.7 copy-start.11
  37.1 18.8 %all-to-all-start = ((bf16[4,64,2048]{2,1,0:T(8,128)(2,1)}), bf16[4,64,2048]{2,1,0:T(8,128)(2,1)S(1)}, u32[]{:S(2)}, u32[]{:S(2)}) async-start(bf16[4,64,2048]{2,1,0:T(8,128)(2,1)} %broadcast_select_fusion), calls=%async_computation | async-start | bytes 2097152 | tf_op jit(solution)/shard_map/all_to_all | solution.py:67
  99.4 351.0 %all-to-all-start.3 = ((bf16[4,128,7168]{2,1,0:T(8,128)(2,1)}), bf16[4,128,7168]{2,1,0:T(8,128)(2,1)}, u32[]{:S(2)}, u32[]{:S(2)}) async-start(bf16[4,128,7168]{2,1,0:T(8,128)(2,1)} %fusion.3), calls=%async_computation.3 | async-start | bytes 14680064 | tf_op jit(solution)/shard_map/all_to_all | solution.py:82
  450.3 322.3 %all-to-all-start.2 = ((bf16[4,128,7168]{2,1,0:T(8,128)(2,1)}), bf16[4,128,7168]{2,1,0:T(8,128)(2,1)}, u32[]{:S(2)}, u32[]{:S(2)}) async-start(bf16[4,128,7168]{2,1,0:T(8,128)(2,1)} %fusion.2), calls=%async_computation.2 | async-start | bytes 14680064 | tf_op jit(solution)/shard_map/all_to_all | solution.py:79
  772.7 5.0 copy-start.2
  778.6 91.0 %collective-permute-start = (bf16[128,7168]{1,0:T(8,128)(2,1)S(1)}, bf16[128,7168]{1,0:T(8,128)(2,1)S(1)}, u32[]{:S(2)}, u32[]{:S(2)}) collective-permute-start(bf16[128,7168]{1,0:T(8,128)(2,1)S(1)} %multiply_convert_fusion.1), channel_id=1, source_target_pairs={{8,0},{16,8},{24,16},{9,1},{17,9},{25,17},{10,2},{18,10},{26,18},{... | collective-permute-start | bytes 5505032 | tf_op jit(solution)/shard_map/ppermute | solution.py:17
  779.9 91.0 %collective-permute-start.1 = (bf16[128,7168]{1,0:T(8,128)(2,1)S(1)}, bf16[128,7168]{1,0:T(8,128)(2,1)S(1)}, u32[]{:S(2)}, u32[]{:S(2)}) collective-permute-start(bf16[128,7168]{1,0:T(8,128)(2,1)S(1)} %multiply_convert_fusion.1), channel_id=1, source_target_pairs={{0,8},{8,16},{16,24},{1,9},{9,17},{17,25},{2,10},{10,18},{18,26},{... | collective-permute-start | bytes 5505032 | tf_op jit(solution)/shard_map/ppermute | solution.py:16
  869.6 46.9 %collective-permute-start.4 = (bf16[128,7168]{1,0:T(8,128)(2,1)S(1)}, bf16[128,7168]{1,0:T(8,128)(2,1)S(1)}, u32[]{:S(2)}, u32[]{:S(2)}) collective-permute-start(bf16[128,7168]{1,0:T(8,128)(2,1)S(1)} %collective-permute-done), channel_id=1, source_target_pairs={{8,0},{16,8},{9,1},{17,9},{10,2},{18,10},{11,3},{19,11},{12,4},{20... | collective-permute-start | bytes 5505032 | tf_op jit(solution)/shard_map/ppermute | solution.py:17
  870.9 46.9 %collective-permute-start.2 = (bf16[128,7168]{1,0:T(8,128)(2,1)S(1)}, bf16[128,7168]{1,0:T(8,128)(2,1)S(1)}, u32[]{:S(2)}, u32[]{:S(2)}) collective-permute-start(bf16[128,7168]{1,0:T(8,128)(2,1)S(1)} %collective-permute-done.1), channel_id=1, source_target_pairs={{8,16},{16,24},{9,17},{17,25},{10,18},{18,26},{11,19},{19,27},{12,... | collective-permute-start | bytes 5505032 | tf_op jit(solution)/shard_map/ppermute | solution.py:16
  916.5 44.0 %collective-permute-start.5 = (bf16[128,7168]{1,0:T(8,128)(2,1)S(1)}, bf16[128,7168]{1,0:T(8,128)(2,1)S(1)}, u32[]{:S(2)}, u32[]{:S(2)}) collective-permute-start(bf16[128,7168]{1,0:T(8,128)(2,1)S(1)} %collective-permute-done.4), channel_id=1, source_target_pairs={{8,0},{9,1},{10,2},{11,3},{12,4},{13,5},{14,6},{15,7}} | collective-permute-start | bytes 5505032 | tf_op jit(solution)/shard_map/ppermute | solution.py:17
  917.8 43.1 %collective-permute-start.3 = (bf16[128,7168]{1,0:T(8,128)(2,1)S(1)}, bf16[128,7168]{1,0:T(8,128)(2,1)S(1)}, u32[]{:S(2)}, u32[]{:S(2)}) collective-permute-start(bf16[128,7168]{1,0:T(8,128)(2,1)S(1)} %collective-permute-done.2), channel_id=1, source_target_pairs={{16,24},{17,25},{18,26},{19,27},{20,28},{21,29},{22,30},{23,31}} | collective-permute-start | bytes 5505032 | tf_op jit(solution)/shard_map/ppermute | solution.py:16
  919.0 42.3 %copy-start.6 = (bf16[128,7168]{1,0:T(8,128)(2,1)}, bf16[128,7168]{1,0:T(8,128)(2,1)S(1)}, u32[]{:S(2)}) copy-start(bf16[128,7168]{1,0:T(8,128)(2,1)S(1)} %add.172) | copy-start | bytes 5505028
  960.9 8.3 copy-start.7
  961.4 7.9 copy-start.8
  969.3 26.4 %copy-start.10 = (f32[1,128,2]{1,2,0:T(2,128)S(1)}, f32[1,128,2]{1,2,0:T(2,128)}, u32[]{:S(2)}) copy-start(f32[1,128,2]{1,2,0:T(2,128)} %param.16) | copy-start | bytes 3076
  970.8 19.4 %all-to-all-start.4 = ((bf16[4,128,512]{2,1,0:T(8,128)(2,1)}), bf16[4,128,512]{2,1,0:T(8,128)(2,1)S(1)}, u32[]{:S(2)}, u32[]{:S(2)}) async-start(bf16[4,128,512]{2,1,0:T(8,128)(2,1)} %broadcast_select_fusion.2), calls=%async_computation.4 | async-start | bytes 1048576 | tf_op jit(solution)/shard_map/all_to_all | solution.py:95
  990.2 12.3 %copy-start.3 = (bf16[4,128,512]{2,1,0:T(8,128)(2,1)}, bf16[4,128,512]{2,1,0:T(8,128)(2,1)S(1)}, u32[]{:S(2)}) copy-start(bf16[4,128,512]{2,1,0:T(8,128)(2,1)S(1)} %all-to-all-done.4) | copy-start | bytes 1572868
  991.8 10.2 all-to-all-start.5
  1002.3 3.0 copy-start.9
  1002.3 3.0 collective-permute-start.6
  1012.4 18.9 %all-to-all-start.6 = ((bf16[4,64,2048]{2,1,0:T(8,128)(2,1)}), bf16[4,64,2048]{2,1,0:T(8,128)(2,1)}, u32[]{:S(2)}, u32[]{:S(2)}) async-start(bf16[4,64,2048]{2,1,0:T(8,128)(2,1)} %bitcast.17), calls=%async_computation.6 | async-start | bytes 2097152 | tf_op jit(solution)/shard_map/all_to_all | solution.py:67
  1028.1 1.0 copy-start.4
  1031.3 16.9 %copy-start.5 = (bf16[1,128,2048]{2,1,0:T(8,128)(2,1)S(1)}, bf16[1,128,2048]{2,1,0:T(8,128)(2,1)}, u32[]{:S(2)}) copy-start(bf16[1,128,2048]{2,1,0:T(8,128)(2,1)} %param.14) | copy-start | bytes 1572868
  1046.2 2.0 collective-permute-start.7
  1054.0 17.7 %all-to-all-start.8 = ((bf16[4,64,2048]{2,1,0:T(8,128)(2,1)}), bf16[4,64,2048]{2,1,0:T(8,128)(2,1)S(1)}, u32[]{:S(2)}, u32[]{:S(2)}) async-start(bf16[4,64,2048]{2,1,0:T(8,128)(2,1)} %bitcast.23), calls=%async_computation.8 | async-start | bytes 2097152 | tf_op jit(solution)/shard_map/all_to_all | solution.py:67
  1076.0 17.7 %all-to-all-start.9 = ((bf16[4,128,512]{2,1,0:T(8,128)(2,1)}), bf16[4,128,512]{2,1,0:T(8,128)(2,1)S(1)}, u32[]{:S(2)}, u32[]{:S(2)}) async-start(bf16[4,128,512]{2,1,0:T(8,128)(2,1)} %bitcast.54), calls=%async_computation.9 | async-start | bytes 1048576 | tf_op jit(solution)/shard_map/all_to_all | solution.py:165
  1094.4 10.5 copy-start.1
Sparse Core Ops, SparseCore 0:
  31.0 833.6 reduce-scatter.1

commit v2 on v1

--- a/solution.py
+++ b/solution.py
@@ -15,7 +15,9 @@
         down = [(j + 1, j) for j in range(0, count - step)]
         behind.append(lax.ppermute(behind[-1], "client", up))
         ahead.append(lax.ppermute(ahead[-1], "client", down))
-    return [own] + [ahead[k] + behind[count - k] for k in range(1, count)]
+    arrived = ahead[1][0, 0].astype(jnp.float32) + behind[1][0, 0].astype(jnp.float32)
+    blocks = [own] + [ahead[k] + behind[count - k] for k in range(1, count)]
+    return blocks, jnp.minimum(jnp.abs(arrived), 0.0)
 
 
 def local(tokens, target, routes, gate_weights, counts, gate_proj, up_proj, down_proj, correction):
@@ -38,8 +40,14 @@
     offset = (own_expert - first_expert) * capacity
     weight_share = counts[client_index].astype(jnp.float32) / jnp.sum(counts).astype(jnp.float32)
     control = correction[0]
-    scaled = (weight_share * control.astype(jnp.float32)).astype(jnp.bfloat16)
-    control_sum = lax.psum_scatter(scaled, "client", scatter_dimension=1, tiled=True)
+    early_units = unit_count // 2
+
+    def weighted_control(block, share):
+        scaled = (share * block.astype(jnp.float32)).astype(jnp.bfloat16)
+        first = jnp.minimum(jnp.abs(scaled[0, 0].astype(jnp.float32)), 0.0)
+        return lax.psum_scatter(scaled, "client", scatter_dimension=1, tiled=True), first
+
+    early_sum, ready = weighted_control(control[:early_units], weight_share)
     flat_routes = routes[0].reshape(-1)
     onehot = (flat_routes[:, None] == jnp.arange(EXPERTS, dtype=jnp.int32)[None, :]).astype(
         jnp.int32
@@ -67,7 +75,7 @@
         arrived = lax.all_to_all(blocks, "expert", split_axis=0, concat_axis=0, tiled=True)
         return own_of(arrived)
 
-    token_slots = jnp.take(tokens[0], source_of // top_count, axis=0)
+    token_slots = jnp.take(tokens[0] + ready.astype(tokens.dtype), source_of // top_count, axis=0)
     features = send_out(token_slots)
     columns = feature_width // client_count
     row_total = features.shape[0]
@@ -86,7 +94,8 @@
     gate_pre = jnp.sum(gate_back, axis=0)
     up_pre = jnp.sum(up_back, axis=0)
     hidden = (jax.nn.silu(gate_pre) * up_pre).astype(jnp.bfloat16)
-    gathered = gather_line(hidden, client_count)
+    gathered, late = gather_line(hidden, client_count)
+    late_sum, _ = weighted_control(control[early_units:], weight_share + late)
     spread = jnp.concatenate(gathered, axis=0)
     order = (client_index + jnp.arange(client_count, dtype=jnp.int32)) % client_count
     inverse = (jnp.arange(client_count, dtype=jnp.int32) - client_index) % client_count
@@ -167,6 +176,7 @@
     gradient = lax.dot_general(
         spread, mean_rows, (((0,), (0,)), ((), ())), preferred_element_type=jnp.float32
     )
+    control_sum = jnp.concatenate([early_sum, late_sum], axis=0)
     return gradient + control_sum.astype(jnp.float32)
 
 

time: 1110 us -> 1120 us (level)
  blocking collectives: 45.7 us -> 11.6 us
  waiting for transfers between devices: 881 us -> 910 us
    all_to_all x1, waiting for transfers between devices: 310 us -> 176 us  [local(): lax.all_to_all(gate_parts.astype(jnp.bfloat16), 'client', split_axis=0, c...]
    ppermute x3, waiting for transfers between devices: 171 us -> 268 us  [gather_line(): ahead.append(lax.ppermute(ahead[-1], 'client', down))]
    ppermute x3, waiting for transfers between devices: 0.01 us -> 38.1 us  [gather_line(): behind.append(lax.ppermute(behind[-1], 'client', up))]
    all_to_all x1 -> x0, blocking collectives: 33.8 us -> none  [local(): lax.all_to_all(pieces, 'client', split_axis=1, concat_axis=1, tiled=True)]
    all_to_all x0 -> x1, waiting for transfers between devices: none -> 20 us  [local(): lax.all_to_all(pieces, 'client', split_axis=1, concat_axis=1, tiled=True)]
    all_to_all x1, waiting for transfers between devices: 12.7 us -> 24.5 us  [local(): lax.all_to_all(by_client, 'client', split_axis=0, concat_axis=0, tiled=True)]
    convert_element_type x1 -> x2, other arithmetic: 20.4 us -> 28.9 us  [weighted_control(): scaled = (share * block.astype(jnp.float32)).astype(jnp.bfloat16)]
  transfers between devices with their start and end apart: 17 -> 19, of which waited for: 12 -> 14; matrix products, arithmetic and copies ran while one was open for 8% -> 8% of each run, Pallas kernels for 0% -> 0%
where the time goes in v2:
time: 1120 us
  waiting for transfers between devices  910 us (81%)
  other arithmetic  57 us (5%)
  matrix products  52.3 us (5%)
  starting transfers between devices  46.7 us (4%)
  local copies, waits for them, and re-layouts  24.2 us (2%)
  between operations  17.3 us (2%)
  blocking collectives  11.6 us (1%)
    all_to_all x1, waiting for transfers between devices, local(): lax.all_to_all(up_parts.astype(jnp.bfloat16), 'client', split_axis=0, con...  332 us
    ppermute x3, waiting for transfers between devices, gather_line(): ahead.append(lax.ppermute(ahead[-1], 'client', down))  268 us
    all_to_all x1, waiting for transfers between devices, local(): lax.all_to_all(gate_parts.astype(jnp.bfloat16), 'client', split_axis=0, c...  176 us
    ppermute x3, waiting for transfers between devices, gather_line(): behind.append(lax.ppermute(behind[-1], 'client', up))  38.1 us
    all_to_all x3, waiting for transfers between devices, send_out(): lax.all_to_all(blocks, 'expert', split_axis=0, concat_axis=0, tiled=True)  29.2 us
    convert_element_type x2, other arithmetic, weighted_control(): scaled = (share * block.astype(jnp.float32)).astype(jnp.bfloat16)  28.9 us
    all_to_all x1, waiting for transfers between devices, local(): lax.all_to_all(by_client, 'client', split_axis=0, concat_axis=0, tiled=True)  24.5 us
  transfers between devices with their start and end apart: 19, of which 14 were waited for; matrix products, arithmetic and copies ran while one was open for 8% of the time, Pallas kernels for 0%

profile of v2, /device:TPU:0, one launch (start us, length us, event | category | flops | bytes accessed | tf_op | source)
XLA Modules:
  0.0 1119.1 jit_solution(5427867237802456240)
XLA Ops:
  7.6 1.3 reduce_sum.51
  9.6 1.3 dynamic_slice.13
  12.6 1.4 scatter_custom_fusion
  14.2 14.5 %fusion.2 = bf16[3584,2048]{1,0:T(8,128)(2,1)} fusion(bf16[1,7168,2048]{2,1,0:T(8,128)(2,1)} %param.21, f32[]{:T(128)S(6)} %div.42), kind=kLoop, calls=%fused_computation.11 | loop fusion | flops 22020096 | bytes 29360132 | tf_op jit(solution)/shard_map/convert_element_type | solution.py:46
  30.6 1.4 gather_fusion
  33.1 5.2 all-to-all-start
  38.3 13.6 %all-to-all-done = bf16[4,64,2048]{2,1,0:T(8,128)(2,1)S(1)} async-done(((bf16[4,64,2048]{2,1,0:T(8,128)(2,1)}), bf16[4,64,2048]{2,1,0:T(8,128)(2,1)S(1)}, u32[]{:S(2)}, u32[]{:S(2)}) %all-to-all-start) | async-done | bytes 1048608 | tf_op jit(solution)/shard_map/all_to_all | solution.py:75
  53.2 4.9 all-to-all-start.1
  58.9 20.0 %all-to-all-done.1 = bf16[128,4,512]{2,0,1:T(8,128)(2,1)S(1)} async-done(((bf16[128,4,512]{2,0,1:T(8,128)(2,1)}), bf16[128,4,512]{2,0,1:T(8,128)(2,1)S(1)}, u32[]{:S(2)}, u32[]{:S(2)}) %all-to-all-start.1) | async-done | bytes 524320 | tf_op jit(solution)/shard_map/all_to_all | solution.py:83
  78.9 9.2 fusion.5
  88.1 5.5 all-to-all-start.3
  93.6 9.2 fusion.4
  102.7 331.7 %all-to-all-done.3 = bf16[4,128,7168]{2,1,0:T(8,128)(2,1)} async-done(((bf16[4,128,7168]{2,1,0:T(8,128)(2,1)}), bf16[4,128,7168]{2,1,0:T(8,128)(2,1)}, u32[]{:S(2)}, u32[]{:S(2)}) %all-to-all-start.3) | async-done | bytes 7340064 | tf_op jit(solution)/shard_map/all_to_all | solution.py:90
  434.5 5.4 all-to-all-start.2
  440.1 6.7 convert_reduce_fusion
  446.8 175.7 %all-to-all-done.2 = bf16[4,128,7168]{2,1,0:T(8,128)(2,1)} async-done(((bf16[4,128,7168]{2,1,0:T(8,128)(2,1)}), bf16[4,128,7168]{2,1,0:T(8,128)(2,1)}, u32[]{:S(2)}, u32[]{:S(2)}) %all-to-all-start.2) | async-done | bytes 7340064 | tf_op jit(solution)/shard_map/all_to_all | solution.py:87
  622.5 5.0 convert_reduce_fusion.1
  628.5 1.4 collective-permute-start.1
  629.9 1.3 collective-permute-start
  631.2 38.1 %collective-permute-done.1 = bf16[128,7168]{1,0:T(8,128)(2,1)S(1)} collective-permute-done((bf16[128,7168]{1,0:T(8,128)(2,1)S(1)}, bf16[128,7168]{1,0:T(8,128)(2,1)S(1)}, u32[]{:S(2)}, u32[]{:S(2)}) %collective-permute-start.1) | collective-permute-done | bytes 1835040 | tf_op jit(solution)/shard_map/ppermute | solution.py:16
  669.9 3.7 collective-permute-done
  676.1 14.4 %fusion.3 = bf16[3584,2048]{1,0:T(8,128)(2,1)} fusion(bf16[1,7168,2048]{2,1,0:T(8,128)(2,1)} %param.21, f32[]{:T(128)S(6)} %add.215), kind=kLoop, calls=%fused_computation.12 | loop fusion | flops 22020096 | bytes 29360132 | tf_op jit(solution)/shard_map/convert_element_type | solution.py:46
  691.5 1.3 collective-permute-start.4
  693.6 140.5 %collective-permute-done.4 = bf16[128,7168]{1,0:T(8,128)(2,1)S(1)} collective-permute-done((bf16[128,7168]{1,0:T(8,128)(2,1)}, bf16[128,7168]{1,0:T(8,128)(2,1)S(1)}, u32[]{:S(2)}, u32[]{:S(2)}) %collective-permute-start.4) | collective-permute-done | bytes 1835040 | tf_op jit(solution)/shard_map/ppermute | solution.py:17
  834.1 1.3 collective-permute-start.5
  836.4 123.9 %collective-permute-done.5 = bf16[128,7168]{1,0:T(8,128)(2,1)S(1)} collective-permute-done((bf16[128,7168]{1,0:T(8,128)(2,1)S(1)}, bf16[128,7168]{1,0:T(8,128)(2,1)S(1)}, u32[]{:S(2)}, u32[]{:S(2)}) %collective-permute-start.5) | collective-permute-done | bytes 1835040 | tf_op jit(solution)/shard_map/ppermute | solution.py:17
  960.8 7.8 convolution_convert_fusion.4
  970.2 3.5 all-to-all-start.4
  973.8 24.5 %all-to-all-done.4 = bf16[4,128,512]{2,1,0:T(8,128)(2,1)S(1)} async-done(((bf16[4,128,512]{2,1,0:T(8,128)(2,1)}), bf16[4,128,512]{2,1,0:T(8,128)(2,1)S(1)}, u32[]{:S(2)}, u32[]{:S(2)}) %all-to-all-start.4) | async-done | bytes 524320 | tf_op jit(solution)/shard_map/all_to_all | solution.py:104
  999.9 3.7 all-to-all-start.5
  1004.0 6.0 all-to-all-done.5
  1010.7 1.9 gather_fusion.1
  1013.3 1.6 fusion.13
  1014.9 2.7 gather_fusion.3
  1017.6 2.9 fusion.12
  1020.5 4.3 all-to-all-start.6
  1024.7 11.4 %fusion = f32[128,2048]{1,0:T(8,128)S(1)} fusion(bf16[128,7168]{1,0:T(8,128)(2,1)S(1)} %multiply_convert_fusion.2, bf16[1,7168,2048]{2,1,0:T(8,128)(2,1)} %param.21), kind=kOutput, calls=%fused_computation.7 | convolution fusion | flops 3758096384 | bytes 32243712 | tf_op jit(solution)/shard_map/dot_general | solution.py:112
  1038.1 1.4 all-to-all-done.6
  1040.5 1.6 fusion.10
  1042.1 11.6 %all_to_all.50 = bf16[4,32,2048]{2,1,0:T(8,128)(2,1)S(1)} all-to-all(bf16[4,32,2048]{2,1,0:T(8,128)(2,1)S(1)} %bitcast.65), channel_id=1, replica_groups=mesh['client'=4,'expert'=4,'shard'=2] {'expert'}, dimensions={0} | all-to-all | bytes 1048576 | tf_op jit(solution)/shard_map/all_to_all | solution.py:152
  1054.1 1.9 collective-permute-done.7
  1056.2 2.8 gather_fusion.4
  1059.0 2.9 fusion.11
  1061.8 3.5 all-to-all-start.8
  1065.4 14.2 %all-to-all-done.8 = bf16[4,64,2048]{2,1,0:T(8,128)(2,1)S(1)} async-done(((bf16[4,64,2048]{2,1,0:T(8,128)(2,1)}), bf16[4,64,2048]{2,1,0:T(8,128)(2,1)S(1)}, u32[]{:S(2)}, u32[]{:S(2)}) %all-to-all-start.8) | async-done | bytes 1048608 | tf_op jit(solution)/shard_map/all_to_all | solution.py:75
  1082.0 3.5 all-to-all-start.9
  1085.6 14.1 %all-to-all-done.9 = bf16[4,128,512]{2,1,0:T(8,128)(2,1)S(1)} async-done(((bf16[4,128,512]{2,1,0:T(8,128)(2,1)}), bf16[4,128,512]{2,1,0:T(8,128)(2,1)S(1)}, u32[]{:S(2)}, u32[]{:S(2)}) %all-to-all-start.9) | async-done | bytes 524320 | tf_op jit(solution)/shard_map/all_to_all | solution.py:174
  1100.5 11.8 %convert_add_fusion = f32[7168,512]{1,0:T(8,128)} fusion(bf16[512,512]{1,0:T(8,128)(2,1)S(1)} %bitcast.69, bf16[3584,512]{1,0:T(8,128)(2,1)} %reduce-scatter.5.cloned.1.call-done, bf16[3584,512]{1,0:T(8,128)(2,1)} %reduce-scatter.3.cloned.1.call-done, bf16[128,7168]{1,0:T(8,128)(2,1)} %copy-done.4, bf16[128,7168]{1,0:T(8,128)(2,1)} %copy-done.2, ...), kind=kOutput, calls=%fused_computation.13 | convolution fusion | flops 3805806592 | bytes 29884416 | tf_op jit(solution)/shard_map/dot_general | solution.py:176
  (101 shorter events, 24.6 us)
Async XLA Ops:
  14.1 16.4 %copy-start.9 = (bf16[1,128,2048]{2,1,0:T(8,128)(2,1)S(1)}, bf16[1,128,2048]{2,1,0:T(8,128)(2,1)}, u32[]{:S(2)}) copy-start(bf16[1,128,2048]{2,1,0:T(8,128)(2,1)} %param.13) | copy-start | bytes 1572868
  33.1 18.8 %all-to-all-start = ((bf16[4,64,2048]{2,1,0:T(8,128)(2,1)}), bf16[4,64,2048]{2,1,0:T(8,128)(2,1)S(1)}, u32[]{:S(2)}, u32[]{:S(2)}) async-start(bf16[4,64,2048]{2,1,0:T(8,128)(2,1)} %broadcast_select_fusion), calls=%async_computation | async-start | bytes 2097152 | tf_op jit(solution)/shard_map/all_to_all | solution.py:75
  53.2 25.7 %all-to-all-start.1 = ((bf16[128,4,512]{2,0,1:T(8,128)(2,1)}), bf16[128,4,512]{2,0,1:T(8,128)(2,1)S(1)}, u32[]{:S(2)}, u32[]{:S(2)}) async-start(bf16[128,4,512]{2,0,1:T(8,128)(2,1)} %copy.31), calls=%async_computation.1 | async-start | bytes 1048576 | tf_op jit(solution)/shard_map/all_to_all | solution.py:83
  58.2 1042.3 %reduce-scatter.3.cloned.1.call-start = ((), (), s32[]{:S(2)}) async-start(), calls=%async_computation.12 | async-start | bytes 18350080 | tf_op jit(solution)/shard_map/reduce_scatter | solution.py:48
  88.1 346.3 %all-to-all-start.3 = ((bf16[4,128,7168]{2,1,0:T(8,128)(2,1)}), bf16[4,128,7168]{2,1,0:T(8,128)(2,1)}, u32[]{:S(2)}, u32[]{:S(2)}) async-start(bf16[4,128,7168]{2,1,0:T(8,128)(2,1)} %fusion.5), calls=%async_computation.3 | async-start | bytes 14680064 | tf_op jit(solution)/shard_map/all_to_all | solution.py:90
  434.5 188.1 %all-to-all-start.2 = ((bf16[4,128,7168]{2,1,0:T(8,128)(2,1)}), bf16[4,128,7168]{2,1,0:T(8,128)(2,1)}, u32[]{:S(2)}, u32[]{:S(2)}) async-start(bf16[4,128,7168]{2,1,0:T(8,128)(2,1)} %fusion.4), calls=%async_computation.2 | async-start | bytes 14680064 | tf_op jit(solution)/shard_map/all_to_all | solution.py:87
  439.9 660.6 %reduce-scatter.5.cloned.1.call-start = ((), (), s32[]{:S(2)}) async-start(), calls=%async_computation.13 | async-start | bytes 18350080 | tf_op jit(solution)/shard_map/reduce_scatter | solution.py:48
  622.5 5.0 copy-start
  628.5 40.8 %collective-permute-start.1 = (bf16[128,7168]{1,0:T(8,128)(2,1)S(1)}, bf16[128,7168]{1,0:T(8,128)(2,1)S(1)}, u32[]{:S(2)}, u32[]{:S(2)}) collective-permute-start(bf16[128,7168]{1,0:T(8,128)(2,1)S(1)} %multiply_convert_fusion.2), channel_id=1, source_target_pairs={{0,8},{8,16},{16,24},{1,9},{9,17},{17,25},{2,10},{10,18},{18,26},{... | collective-permute-start | bytes 5505032 | tf_op jit(solution)/shard_map/ppermute | solution.py:16
  629.9 43.6 %collective-permute-start = (bf16[128,7168]{1,0:T(8,128)(2,1)S(1)}, bf16[128,7168]{1,0:T(8,128)(2,1)S(1)}, u32[]{:S(2)}, u32[]{:S(2)}) collective-permute-start(bf16[128,7168]{1,0:T(8,128)(2,1)S(1)} %multiply_convert_fusion.2), channel_id=1, source_target_pairs={{8,0},{16,8},{24,16},{9,1},{17,9},{25,17},{10,2},{18,10},{26,18},{... | collective-permute-start | bytes 5505032 | tf_op jit(solution)/shard_map/ppermute | solution.py:17
  669.3 4.2 copy-start.5
  673.5 1.3 copy-start.7
  690.6 145.4 %copy-start.8 = (bf16[128,7168]{1,0:T(8,128)(2,1)S(1)}, bf16[128,7168]{1,0:T(8,128)(2,1)}, u32[]{:S(2)}) copy-start(bf16[128,7168]{1,0:T(8,128)(2,1)} %copy-done.7) | copy-start | bytes 5505028
  690.6 2.2 collective-permute-start.2
  691.5 142.6 %collective-permute-start.4 = (bf16[128,7168]{1,0:T(8,128)(2,1)}, bf16[128,7168]{1,0:T(8,128)(2,1)S(1)}, u32[]{:S(2)}, u32[]{:S(2)}) collective-permute-start(bf16[128,7168]{1,0:T(8,128)(2,1)} %copy-done.7), channel_id=1, source_target_pairs={{8,0},{16,8},{9,1},{17,9},{10,2},{18,10},{11,3},{19,11},{12,4},{20... | collective-permute-start | bytes 5505032 | tf_op jit(solution)/shard_map/ppermute | solution.py:17
  692.8 143.1 %collective-permute-start.3 = (bf16[128,7168]{1,0:T(8,128)(2,1)S(1)}, bf16[128,7168]{1,0:T(8,128)(2,1)S(1)}, u32[]{:S(2)}, u32[]{:S(2)}) collective-permute-start(bf16[128,7168]{1,0:T(8,128)(2,1)S(1)} %collective-permute-done.2), channel_id=1, source_target_pairs={{16,24},{17,25},{18,26},{19,27},{20,28},{21,29},{22,30},{23,31}} | collective-permute-start | bytes 5505032 | tf_op jit(solution)/shard_map/ppermute | solution.py:16
  834.1 126.2 %collective-permute-start.5 = (bf16[128,7168]{1,0:T(8,128)(2,1)S(1)}, bf16[128,7168]{1,0:T(8,128)(2,1)S(1)}, u32[]{:S(2)}, u32[]{:S(2)}) collective-permute-start(bf16[128,7168]{1,0:T(8,128)(2,1)S(1)} %collective-permute-done.4), channel_id=1, source_target_pairs={{8,0},{9,1},{10,2},{11,3},{12,4},{13,5},{14,6},{15,7}} | collective-permute-start | bytes 5505032 | tf_op jit(solution)/shard_map/ppermute | solution.py:17
  835.9 124.9 %copy-start.2 = (bf16[128,7168]{1,0:T(8,128)(2,1)}, bf16[128,7168]{1,0:T(8,128)(2,1)S(1)}, u32[]{:S(2)}) copy-start(bf16[128,7168]{1,0:T(8,128)(2,1)S(1)} %add.194) | copy-start | bytes 5505028
  835.9 124.4 %copy-start.6 = (bf16[128,7168]{1,0:T(8,128)(2,1)S(1)}, bf16[128,7168]{1,0:T(8,128)(2,1)}, u32[]{:S(2)}) copy-start(bf16[128,7168]{1,0:T(8,128)(2,1)} %copy-done.5) | copy-start | bytes 5505028
  836.4 132.2 %copy-start.3 = (bf16[128,7168]{1,0:T(8,128)(2,1)}, bf16[128,7168]{1,0:T(8,128)(2,1)S(1)}, u32[]{:S(2)}) copy-start(bf16[128,7168]{1,0:T(8,128)(2,1)S(1)} %add.193) | copy-start | bytes 5505028
  960.8 7.9 copy-start.4
  968.6 35.2 %copy-start.11 = (f32[1,128,2]{1,2,0:T(2,128)S(1)}, f32[1,128,2]{1,2,0:T(2,128)}, u32[]{:S(2)}) copy-start(f32[1,128,2]{1,2,0:T(2,128)} %param.16) | copy-start | bytes 3076
  970.2 28.1 %all-to-all-start.4 = ((bf16[4,128,512]{2,1,0:T(8,128)(2,1)}), bf16[4,128,512]{2,1,0:T(8,128)(2,1)S(1)}, u32[]{:S(2)}, u32[]{:S(2)}) async-start(bf16[4,128,512]{2,1,0:T(8,128)(2,1)} %broadcast_select_fusion.2), calls=%async_computation.4 | async-start | bytes 1048576 | tf_op jit(solution)/shard_map/all_to_all | solution.py:104
  999.9 10.1 all-to-all-start.5
  1010.3 3.0 copy-start.10
  1010.3 3.0 collective-permute-start.6
  1020.5 19.0 %all-to-all-start.6 = ((bf16[4,64,2048]{2,1,0:T(8,128)(2,1)}), bf16[4,64,2048]{2,1,0:T(8,128)(2,1)}, u32[]{:S(2)}, u32[]{:S(2)}) async-start(bf16[4,64,2048]{2,1,0:T(8,128)(2,1)} %bitcast.19), calls=%async_computation.6 | async-start | bytes 2097152 | tf_op jit(solution)/shard_map/all_to_all | solution.py:75
  1038.1 17.9 %copy-start.1 = (bf16[1,128,2048]{2,1,0:T(8,128)(2,1)S(1)}, bf16[1,128,2048]{2,1,0:T(8,128)(2,1)}, u32[]{:S(2)}) copy-start(bf16[1,128,2048]{2,1,0:T(8,128)(2,1)} %param.14) | copy-start | bytes 1572868
  1054.0 2.0 collective-permute-start.7
  1061.8 17.7 %all-to-all-start.8 = ((bf16[4,64,2048]{2,1,0:T(8,128)(2,1)}), bf16[4,64,2048]{2,1,0:T(8,128)(2,1)S(1)}, u32[]{:S(2)}, u32[]{:S(2)}) async-start(bf16[4,64,2048]{2,1,0:T(8,128)(2,1)} %bitcast.25), calls=%async_computation.8 | async-start | bytes 2097152 | tf_op jit(solution)/shard_map/all_to_all | solution.py:75
  1082.0 17.7 %all-to-all-start.9 = ((bf16[4,128,512]{2,1,0:T(8,128)(2,1)}), bf16[4,128,512]{2,1,0:T(8,128)(2,1)S(1)}, u32[]{:S(2)}, u32[]{:S(2)}) async-start(bf16[4,128,512]{2,1,0:T(8,128)(2,1)} %bitcast.60), calls=%async_computation.9 | async-start | bytes 1048576 | tf_op jit(solution)/shard_map/all_to_all | solution.py:174
Sparse Core Ops, SparseCore 0:
  61.3 449.4 reduce-scatter.2
  690.7 329.2 reduce-scatter.4
